TPU v7x, 32 devices: a whole 2x2x4 slice. The times are simulated.
32 devices in a mesh: grp: 1, gx: 32 (over z, y, x, core), gy: 1.
Axes of the slice: x: 2, y: 2, z: 4, core: 2. Of those that a mesh axis runs over, the one named last changes fastest.
Arguments:
- incident: float32 [2, 16, 128, 128], P('grp', None, 'gx', 'gy'), may hold values from -6 to 6
- material: int32 [16, 128, 128], P('grp', 'gx', 'gy'), may hold values from 0 to 7
- contrast: float32 [8, 2], P('grp'), may hold values from 0.1 to 1.2
- w_first: bfloat16 [32, 4, 3, 3, 3], replicated, may hold values from -0.625 to 0.625
- w_middle: bfloat16 [32, 32, 3, 3, 3], replicated, may hold values from -0.21875 to 0.21875
- w_last: bfloat16 [2, 32, 3, 3, 3], replicated, may hold values from -0.21875 to 0.21875
- z_kernel: float32 [2, 16, 16], P('grp'), may hold values from -1 to 1
- spectral: float32 [2, 128, 128], P('grp', 'gx'), may hold values from -3 to 3
Outputs:
- total_field: float32 [2, 16, 128, 128], P('grp', None, 'gx', 'gy')
Inputs may be any that keep to these rules, and one draw needn't show every extreme that they name: `material`: selects a row of contrast.
All inputs are finite; a program needn't handle non-finite values.
Results may differ from a plain program's by a relative error of at most 0.0013.
Values may be sent and summed in bfloat16 or wider, within the bound.
A program may use at most 64 MiB of HBM per device.

v0:
```python
import math

import jax
import jax.numpy as jnp
from jax import lax
from jax.sharding import PartitionSpec as P


def padded_2(x, sides, width):
    for axis, dim in sides:
        count, length = (lax.axis_size(axis), x.shape[dim])
        up = [(i, (i + 1) % count) for i in range(count)]
        down = [(j, i) for i, j in up]
        last = lax.slice_in_dim(x, length - width, length, axis=dim)
        leading = lax.slice_in_dim(x, 0, width, axis=dim)
        before = lax.ppermute(last, axis, up)
        after = lax.ppermute(leading, axis, down)
        x = jnp.concatenate([before, x, after], axis=dim)
    return x


def conv_layer(values, weights):
    return lax.conv_general_dilated(
        values[None],
        weights,
        (1, 1, 1),
        ((1, 1), (0, 0), (0, 0)),
        dimension_numbers=("NCDHW", "OIDHW", "NCDHW"),
        preferred_element_type=jnp.float32,
    )[0]


def activate(values):
    return jax.nn.gelu(values, approximate=False).astype(jnp.bfloat16)


def dft_tables(length):
    positions = jnp.arange(length, dtype=jnp.int32)
    product = positions[:, None] * positions[None, :] % length
    angle = product.astype(jnp.float32) * (2.0 * math.pi / length)
    return (jnp.cos(angle), jnp.sin(angle))


def green_apply(source, z_kernel, spectral):
    high = lax.Precision.HIGHEST
    kr, ki = (z_kernel[0], z_kernel[1])
    lre = jnp.einsum("zw,wxy->zxy", kr, source[0], precision=high) - jnp.einsum(
        "zw,wxy->zxy", ki, source[1], precision=high
    )
    lim = jnp.einsum("zw,wxy->zxy", kr, source[1], precision=high) + jnp.einsum(
        "zw,wxy->zxy", ki, source[0], precision=high
    )
    columns = lax.all_to_all(jnp.stack([lre, lim]), "gy", split_axis=1, concat_axis=3, tiled=True)
    count_y = columns.shape[3]
    cos_y, sin_y = dft_tables(count_y)
    fwd_re = jnp.dot(columns[0], cos_y, precision=high) + jnp.dot(columns[1], sin_y, precision=high)
    fwd_im = jnp.dot(columns[1], cos_y, precision=high) - jnp.dot(columns[0], sin_y, precision=high)
    count_x = columns.shape[2] * lax.axis_size("gx")
    cos_x, sin_x = dft_tables(count_x)
    piece = lax.all_to_all(
        jnp.stack([fwd_re, fwd_im]), "gx", split_axis=3, concat_axis=2, tiled=True
    )
    ar = jnp.einsum("zxk,xq->zkq", piece[0], cos_x, precision=high) + jnp.einsum(
        "zxk,xq->zkq", piece[1], sin_x, precision=high
    )
    ai = jnp.einsum("zxk,xq->zkq", piece[1], cos_x, precision=high) - jnp.einsum(
        "zxk,xq->zkq", piece[0], sin_x, precision=high
    )
    br = spectral[0] * ar - spectral[1] * ai
    bi = spectral[0] * ai + spectral[1] * ar
    gr = jnp.einsum("zkq,qx->zxk", br, cos_x, precision=high) - jnp.einsum(
        "zkq,qx->zxk", bi, sin_x, precision=high
    )
    gi = jnp.einsum("zkq,qx->zxk", bi, cos_x, precision=high) + jnp.einsum(
        "zkq,qx->zxk", br, sin_x, precision=high
    )
    spread = jnp.stack([gr, gi]) / count_x
    rows = lax.all_to_all(spread, "gx", split_axis=2, concat_axis=3, tiled=True)
    inv_re = jnp.dot(rows[0], cos_y, precision=high) - jnp.dot(rows[1], sin_y, precision=high)
    inv_im = jnp.dot(rows[1], cos_y, precision=high) + jnp.dot(rows[0], sin_y, precision=high)
    scattered = jnp.stack([inv_re, inv_im]) / count_y
    return lax.all_to_all(scattered, "gy", split_axis=3, concat_axis=1, tiled=True)


def per_device(incident, material, contrast, w_first, w_middle, w_last, z_kernel, spectral):
    high = lax.Precision.HIGHEST
    classes = contrast.shape[0]
    selector = (material[None] == jnp.arange(classes, dtype=jnp.int32)[:, None, None, None]).astype(
        jnp.float32
    )
    chi_re = jnp.einsum("k,kzxy->zxy", contrast[:, 0], selector, precision=high)
    chi_im = jnp.einsum("k,kzxy->zxy", contrast[:, 1], selector, precision=high)
    field = incident
    pol_re = chi_re * field[0] - chi_im * field[1]
    pol_im = chi_re * field[1] + chi_im * field[0]
    features = jnp.stack([field[0], field[1], pol_re, pol_im]).astype(jnp.bfloat16)
    padded = padded_2(features, (("gx", 2), ("gy", 3)), 3)
    hidden = activate(conv_layer(padded, w_first))
    hidden = activate(conv_layer(hidden, w_middle))
    correction = conv_layer(hidden, w_last)
    source = jnp.stack([pol_re, pol_im]) + correction
    field = incident + green_apply(source, z_kernel, spectral)
    return field


def solution(mesh):
    placed = (
        P("grp", None, "gx", "gy"),
        P("grp", "gx", "gy"),
        P("grp", None),
        P(),
        P(),
        P(),
        P("grp", None, None),
        P("grp", "gx", None),
    )
    return jax.shard_map(
        per_device,
        mesh=mesh,
        in_specs=placed,
        out_specs=P("grp", None, "gx", "gy"),
        check_vma=False,
    )
```

profile of v0, /device:TPU:0, one launch (start us, length us, event | category | flops | bytes accessed | tf_op | source)
XLA Modules:
  0.0 264.7 jit_solution(12250235178235497739)
XLA Ops:
  0.0 0.9 iota_compare_fusion.3
  0.9 0.9 fusion.60
  1.8 0.9 fusion.62
  2.8 0.8 copy.97
  3.6 0.9 convert.9
  5.8 6.0 %collective-permute-start.1 = (bf16[4,16,3,128]{3,2,1,0:T(4,128)(2,1)S(1)}, bf16[4,16,3,128]{3,2,1,0:T(4,128)(2,1)S(1)}, u32[]{:S(2)}, u32[]{:S(2)}) collective-permute-start(bf16[4,16,3,128]{3,2,1,0:T(4,128)(2,1)S(1)} %get-tuple-element.18), channel_id=1, source_target_pairs={{1,0},{2,1},{3,2},{4,3},{5,4},{6,5},{7,6},{8,7},{9,8},{10,9},{11,1... | collective-permute-start | bytes 147464 | tf_op jit(solution)/shard_map/ppermute | solution.py:17
  11.7 2.0 collective-permute-done
  14.1 0.8 maximum_bitcast_fusion
  15.0 1.1 reshape.36
  16.1 5.2 %copy.78 = bf16[4,16,10,1,8,17]{4,0,5,2,1,3:T(4,128)(2,1)} copy(bf16[4,16,10,1,8,17]{5,4,2,1,0,3:T(8,128)(2,1)S(1)} %reshape.36) | data formatting | bytes 348160 | tf_op jit(solution)/shard_map/conv_general_dilated | solution.py:23
  21.3 1.2 slice.99
  22.5 39.5 %select_bitcast_fusion = bf16[16,8,1,8,17,32]{5,3,4,1,0,2:T(8,128)(2,1)S(1)} fusion(pred[8,17]{0,1:T(8,128)(4,1)S(1)} %copy-done.9, bf16[32,4,3,3,3]{0,1,4,3,2:T(4,128)(2,1)S(1)} %copy-done.6, bf16[4,16,10,1,7,2]{4,0,5,2,1,3:T(4,128)(2,1)S(1)} %slice.99, bf16[4,16,10,1,8,17]{4,0,5,2,1,3:T(4,128)(2,1)} %copy.78), kind=kOutput, calls=%fused_computation.50 | convolution fusion | flops 153217024 | bytes 1313160 | tf_op jit(solution)/shard_map/conv_general_dilated | solution.py:23
  62.3 25.2 %select_bitcast_fusion.1 = bf16[16,6,1,8,17,32]{5,3,4,1,0,2:T(8,128)(2,1)S(1)} fusion(pred[8,17]{0,1:T(8,128)(4,1)S(1)} %copy-done.8, bf16[32,32,3,3,3]{1,0,4,3,2:T(8,128)(2,1)S(1)} %copy-done, bf16[16,8,1,7,2,32]{5,3,4,1,0,2:T(8,128)(2,1)S(1)} %slice.100, bf16[16,8,1,8,17,32]{5,3,4,1,0,2:T(8,128)(2,1)S(1)} %select_bitcast_fusion), kind=kOutput, calls=%fused_computation.54 | convolution fusion | flops 723173376 | bytes 2119816 | tf_op jit(solution)/shard_map/conv_general_dilated | solution.py:23
  87.7 137.1 %fusion.36 = f32[16,4,8,17,2]{2,4,3,1,0:T(2,128)S(1)} fusion(bf16[2,32,3,3,3]{1,0,4,3,2:T(2,128)(2,1)S(1)} %copy-done.7, bf16[16,6,1,7,2,32]{5,3,4,1,0,2:T(8,128)(2,1)S(1)} %slice.101, bf16[16,6,1,8,17,32]{5,3,4,1,0,2:T(8,128)(2,1)S(1)} %select_bitcast_fusion.1), kind=kOutput, calls=%fused_computation.53 | convolution fusion | flops 31629312 | bytes 994688 | tf_op jit(solution)/shard_map/conv_general_dilated | solution.py:23
  224.7 1.0 copy.112
  228.7 1.1 reshape.37
  229.7 5.7 %all-to-all-start = ((f32[32,1,512]{2,1,0:T(1,128)}), f32[32,1,512]{2,1,0:T(1,128)S(1)}, u32[]{:S(2)}, u32[]{:S(2)}) async-start(f32[32,1,512]{2,1,0:T(1,128)} %reshape.37), calls=%async_computation | async-start | bytes 131072 | tf_op jit(solution)/shard_map/all_to_all | solution.py:60
  235.4 7.4 %all-to-all-done = f32[32,1,512]{2,1,0:T(1,128)S(1)} async-done(((f32[32,1,512]{2,1,0:T(1,128)}), f32[32,1,512]{2,1,0:T(1,128)S(1)}, u32[]{:S(2)}, u32[]{:S(2)}) %all-to-all-start) | async-done | bytes 65568 | tf_op jit(solution)/shard_map/all_to_all | solution.py:60
  243.3 0.8 reduce
  247.0 0.6 convolution_add_fusion.2
  250.2 9.1 %all_to_all.30 = f32[32,1,512]{2,1,0:T(1,128)S(1)} all-to-all(f32[32,1,512]{2,1,0:T(1,128)S(1)} %reshape.39), channel_id=1, replica_groups=mesh['grp'=1,'gx'=32,'gy'=1] {'gx'}, dimensions={0} | all-to-all | bytes 131072 | tf_op jit(solution)/shard_map/all_to_all | solution.py:78
  259.3 0.8 reduce.1
  262.3 0.6 fusion.53
  263.7 0.7 copy.98
  (74 shorter events, 13.5 us)
Async XLA Ops:
  0.0 62.2 %copy-start = (bf16[32,32,3,3,3]{1,0,4,3,2:T(8,128)(2,1)S(1)}, bf16[32,32,3,3,3]{1,0,4,3,2:T(8,128)(2,1)}, u32[]{:S(2)}) copy-start(bf16[32,32,3,3,3]{1,0,4,3,2:T(8,128)(2,1)} %param.12) | copy-start | bytes 165892
  5.3 8.5 %collective-permute-start = (bf16[4,16,3,128]{3,2,1,0:T(4,128)(2,1)S(1)}, bf16[4,16,3,128]{3,2,1,0:T(4,128)(2,1)S(1)}, u32[]{:S(2)}, u32[]{:S(2)}) collective-permute-start(bf16[4,16,3,128]{3,2,1,0:T(4,128)(2,1)S(1)} %get-tuple-element.17), channel_id=1, source_target_pairs={{0,1},{1,2},{2,3},{3,4},{4,5},{5,6},{6,7},{7,8},{8,9},{9,10},{10,1... | collective-permute-start | bytes 147464 | tf_op jit(solution)/shard_map/ppermute | solution.py:16
  5.8 8.0 %collective-permute-start.1 = (bf16[4,16,3,128]{3,2,1,0:T(4,128)(2,1)S(1)}, bf16[4,16,3,128]{3,2,1,0:T(4,128)(2,1)S(1)}, u32[]{:S(2)}, u32[]{:S(2)}) collective-permute-start(bf16[4,16,3,128]{3,2,1,0:T(4,128)(2,1)S(1)} %get-tuple-element.18), channel_id=1, source_target_pairs={{1,0},{2,1},{3,2},{4,3},{5,4},{6,5},{7,6},{8,7},{9,8},{10,9},{11,1... | collective-permute-start | bytes 147464 | tf_op jit(solution)/shard_map/ppermute | solution.py:17
  14.1 8.5 %copy-start.6 = (bf16[32,4,3,3,3]{0,1,4,3,2:T(4,128)(2,1)S(1)}, bf16[32,4,3,3,3]{0,1,4,3,2:T(4,128)(2,1)}, u32[]{:S(2)}) copy-start(bf16[32,4,3,3,3]{0,1,4,3,2:T(4,128)(2,1)} %param.11) | copy-start | bytes 20740
  14.1 8.4 %copy-start.9 = (pred[8,17]{0,1:T(8,128)(4,1)S(1)}, pred[8,17]{0,1:T(8,128)(4,1)}, u32[]{:S(2)}) copy-start(pred[8,17]{0,1:T(8,128)(4,1)} %constant.30) | copy-start | bytes 412
  14.1 0.1 collective-permute-start.2
  22.5 39.7 %copy-start.8 = (pred[8,17]{0,1:T(8,128)(4,1)S(1)}, pred[8,17]{0,1:T(8,128)(4,1)}, u32[]{:S(2)}) copy-start(pred[8,17]{0,1:T(8,128)(4,1)} %constant.29) | copy-start | bytes 412
  62.2 25.4 %copy-start.7 = (bf16[2,32,3,3,3]{1,0,4,3,2:T(2,128)(2,1)S(1)}, bf16[2,32,3,3,3]{1,0,4,3,2:T(2,128)(2,1)}, u32[]{:S(2)}) copy-start(bf16[2,32,3,3,3]{1,0,4,3,2:T(2,128)(2,1)} %param.13) | copy-start | bytes 10372
  87.6 138.3 %copy-start.2 = (f32[1,16,4,128]{3,1,2,0:T(8,128)S(1)}, f32[1,16,4,128]{3,1,2,0:T(8,128)}, u32[]{:S(2)}) copy-start(f32[1,16,4,128]{3,1,2,0:T(8,128)} %get-tuple-element.6) | copy-start | bytes 98308
  87.6 138.3 %copy-start.3 = (f32[1,16,4,128]{3,1,2,0:T(8,128)S(1)}, f32[1,16,4,128]{3,1,2,0:T(8,128)}, u32[]{:S(2)}) copy-start(f32[1,16,4,128]{3,1,2,0:T(8,128)} %get-tuple-element.16) | copy-start | bytes 98308
  87.6 138.3 %copy-start.4 = (f32[2,16,16]{2,1,0:T(8,128)S(1)}, f32[2,16,16]{2,1,0:T(8,128)}, u32[]{:S(2)}) copy-start(f32[2,16,16]{2,1,0:T(8,128)} %param.14) | copy-start | bytes 6148
  224.7 10.7 %copy-start.5 = (f32[2,4,128]{2,1,0:T(4,128)S(1)}, f32[2,4,128]{2,1,0:T(4,128)}, u32[]{:S(2)}) copy-start(f32[2,4,128]{2,1,0:T(4,128)} %param.15) | copy-start | bytes 12292
  229.7 13.1 %all-to-all-start = ((f32[32,1,512]{2,1,0:T(1,128)}), f32[32,1,512]{2,1,0:T(1,128)S(1)}, u32[]{:S(2)}, u32[]{:S(2)}) async-start(f32[32,1,512]{2,1,0:T(1,128)} %reshape.37), calls=%async_computation | async-start | bytes 131072 | tf_op jit(solution)/shard_map/all_to_all | solution.py:60
  245.7 18.0 %copy-start.1 = (f32[2,16,4,128]{3,2,1,0:T(4,128)S(1)}, f32[2,16,4,128]{3,2,1,0:T(4,128)}, u32[]{:S(2)}) copy-start(f32[2,16,4,128]{3,2,1,0:T(4,128)} %param.8) | copy-start | bytes 196612
  (1 other events, 0.0 us)
where the time goes:
time: 268 us; the launch traced here: 265 us
  matrix products  213 us (79%)
  local copies, waits for them, and re-layouts  15 us (6%)
  starting transfers between devices  12.2 us (5%)
  waiting for transfers between devices  9.39 us (4%)
  blocking collectives  9.1 us (3%)
  other arithmetic  5 us (2%)
    conv_general_dilated x3, matrix products, conv_layer(): lax.conv_general_dilated(values[None], weights, (1, 1, 1), ((1, 1), (0, 0...  202 us
    all_to_all x1, blocking collectives, green_apply(): rows = lax.all_to_all(spread, 'gx', split_axis=2, concat_axis=3, tiled=True)  9.1 us
    conv_general_dilated x5, local copies, waits for them, and re-layouts, conv_layer(): lax.conv_general_dilated(values[None], weights, (1, 1, 1), ((1, 1), (0, 0...  8.62 us
    all_to_all x1, waiting for transfers between devices, green_apply(): lax.all_to_all(jnp.stack([fwd_re, fwd_im]), 'gx', split_axis=3, concat_ax...  7.39 us
    ppermute x2, starting transfers between devices, padded_2(): after = lax.ppermute(leading, axis, down)  6 us
    all_to_all x1, starting transfers between devices, green_apply(): lax.all_to_all(jnp.stack([fwd_re, fwd_im]), 'gx', split_axis=3, concat_ax...  5.65 us
  transfers between devices with their start and end apart: 5, of which 2 were waited for; matrix products, arithmetic and copies ran while one was open for 0% of the time, Pallas kernels for 0%

commit v1 on v0

--- a/solution.py
+++ b/solution.py
@@ -1,8 +1,13 @@
+import functools
 import math
 
 import jax
 import jax.numpy as jnp
+import ml_dtypes
+import numpy as np
 from jax import lax
+from jax.experimental import pallas as pl
+from jax.experimental.pallas import tpu as pltpu
 from jax.sharding import PartitionSpec as P
 
 
@@ -103,6 +108,396 @@
     return field
 
 
+def table_arrays(length, local):
+    position = np.arange(length)
+    angle = (position[:, None] * position[None, :] % length) * (2.0 * np.pi / length)
+    cos, sin = np.cos(angle), np.sin(angle)
+    order = position.reshape(length // local, local).T.reshape(-1)
+    full = np.stack(
+        [
+            np.concatenate([cos, sin], axis=1),
+            np.concatenate([cos[:, order], sin[:, order]], axis=1),
+        ]
+    ).astype(np.float32)
+    high = full.astype(ml_dtypes.bfloat16)
+    low = (full - high.astype(np.float32)).astype(ml_dtypes.bfloat16)
+    return np.concatenate([high, low])
+
+
+def split(x):
+    high = x.astype(jnp.bfloat16)
+    return high, (x - high.astype(jnp.float32)).astype(jnp.bfloat16)
+
+
+def mxu(a, b):
+    return jnp.dot(a, b, preferred_element_type=jnp.float32)
+
+
+def dot3(a_high, a_low, b):
+    b_high, b_low = split(b)
+    return mxu(a_high, b_high) + (mxu(a_high, b_low) + mxu(a_low, b_high))
+
+
+def gelu(x):
+    return 0.5 * x * (1.0 + lax.erf(x * math.sqrt(0.5)))
+
+
+def whole_kernel(
+    dims,
+    incident_ref,
+    material_ref,
+    contrast_ref,
+    w1_ref,
+    w2_ref,
+    w3_ref,
+    zk_ref,
+    spectral_ref,
+    tables_ref,
+    out_ref,
+    base1,
+    base2,
+    base3,
+    wt1,
+    wt2,
+    wt3,
+    own,
+    halo_left,
+    halo_right,
+    pol,
+    feat,
+    h1,
+    h2,
+    o3,
+    send_a,
+    recv_a,
+    send_b,
+    recv_b,
+    halo_send,
+    halo_recv,
+    a_send,
+    a_recv,
+    b_send,
+    b_recv,
+):
+    n, nz, nx, ny, hid, classes = dims
+    bf16, f32 = jnp.bfloat16, jnp.float32
+    me = lax.axis_index("gx")
+    right, left = lax.rem(me + 1, n), lax.rem(me + n - 1, n)
+    mesh_id = pl.DeviceIdType.MESH
+
+    barrier = pltpu.get_barrier_semaphore()
+
+    def greet(k, carry):
+        pl.semaphore_signal(
+            barrier, inc=1, device_id={"gx": lax.rem(me + k, n)}, device_id_type=mesh_id
+        )
+        return carry
+
+    lax.fori_loop(1, n, greet, 0)
+
+    for x in range(nx):
+        f0 = incident_ref[0, :, x, :]
+        f1 = incident_ref[1, :, x, :]
+        mat = material_ref[:, x, :]
+        cr = jnp.zeros_like(f0)
+        ci = jnp.zeros_like(f0)
+        for k in range(classes):
+            hit = mat == k
+            cr = jnp.where(hit, contrast_ref[k, 0], cr)
+            ci = jnp.where(hit, contrast_ref[k, 1], ci)
+        pr = cr * f0 - ci * f1
+        pi = cr * f1 + ci * f0
+        pol[0, x] = pr
+        pol[1, x] = pi
+        own[x] = jnp.concatenate([f0, f1, pr, pi], axis=0).astype(bf16)
+
+    pl.semaphore_wait(barrier, n - 1)
+
+    to_right = pltpu.make_async_remote_copy(
+        src_ref=own.at[pl.ds(nx - 3, 3)],
+        dst_ref=halo_left,
+        send_sem=halo_send.at[0],
+        recv_sem=halo_recv.at[0],
+        device_id={"gx": right},
+        device_id_type=mesh_id,
+    )
+    to_left = pltpu.make_async_remote_copy(
+        src_ref=own.at[pl.ds(0, 3)],
+        dst_ref=halo_right,
+        send_sem=halo_send.at[1],
+        recv_sem=halo_recv.at[1],
+        device_id={"gx": left},
+        device_id_type=mesh_id,
+    )
+    to_right.start()
+    to_left.start()
+
+    base1[...] = jnp.zeros_like(base1)
+    base2[...] = jnp.zeros_like(base2)
+    base3[...] = jnp.zeros_like(base3)
+    for a in range(3):
+        for t in range(9):
+            base1[t, :, a, 0:hid] = w1_ref[a * 9 + t].astype(f32)
+            base2[t, :, hid * a : hid * a + hid] = w2_ref[a * 9 + t].astype(f32)
+            b, d = divmod(t, 3)
+            base3[b, 2 * d : 2 * d + 2, hid * a : hid * a + hid] = w3_ref[a * 9 + t].astype(f32)
+
+    wide = jnp.transpose(base1[...].reshape(640, 128))[0:hid]
+    lane = lax.broadcasted_iota(jnp.int32, wide.shape, 1) % nz
+    for z in range(nz):
+        block = wide if z == 1 else pltpu.roll(wide, (z - 1) % 640, 1)
+        if z == 0:
+            block = jnp.where(lane == nz - 1, 0.0, block)
+        if z == nz - 1:
+            block = jnp.where(lane == 0, 0.0, block)
+        wt1[z * hid : z * hid + hid, :] = block.astype(bf16)
+    for t in range(9):
+        narrow = base2[t]
+        for z in range(6):
+            block = narrow if z == 0 else pltpu.roll(narrow, hid * z, 1)
+            wt2[z * hid : z * hid + hid, t * 256 : t * 256 + 256] = block.astype(bf16)
+    lane3 = lax.broadcasted_iota(jnp.int32, (8, 512), 1)
+    for b in range(3):
+        line = base3[b]
+        rows = []
+        for z in range(nz):
+            block = line if z == 1 else pltpu.roll(line, (hid * (z - 1)) % 512, 1)
+            if z == 0:
+                block = jnp.where(lane3 >= 512 - hid, 0.0, block)
+            if z == nz - 1:
+                block = jnp.where(lane3 < hid, 0.0, block)
+            rows.append(block)
+        wt3[:, b * 512 : b * 512 + 512] = jnp.concatenate(rows, axis=0).astype(bf16)
+
+    h1[:, :, 0:hid, :] = jnp.zeros((3, nx + 4, hid, ny), bf16)
+    h1[:, :, (nz + 1) * hid :, :] = jnp.zeros((3, nx + 4, 3 * hid, ny), bf16)
+
+    to_right.wait()
+    to_left.wait()
+
+    def shifted(x):
+        return pltpu.roll(x, 1, 1), x, pltpu.roll(x, ny - 1, 1)
+
+    for x in range(nx + 6):
+        if x < 3:
+            piece = halo_left[x]
+        elif x < nx + 3:
+            piece = own[x - 3]
+        else:
+            piece = halo_right[x - nx - 3]
+        for d, moved in enumerate(shifted(piece.astype(f32))):
+            feat[d, x] = moved.astype(bf16)
+
+    def pair(ref, d, x, rows):
+        return jnp.concatenate([ref[d, x, rows, :], ref[d, x + 1, rows, :]], axis=1)
+
+    def first(i, carry):
+        x = 2 * i
+        parts = [pair(feat, d, x + b, slice(None)) for b in range(3) for d in range(3)]
+        hidden = gelu(mxu(wt1[...], jnp.concatenate(parts + [parts[0]], axis=0)))
+        for half in range(2):
+            for d, moved in enumerate(shifted(hidden[:, half * ny : half * ny + ny])):
+                h1[d, x + half, hid : (nz + 1) * hid, :] = moved.astype(bf16)
+        return carry
+
+    lax.fori_loop(0, (nx + 4) // 2, first, 0)
+
+    def second(i, carry):
+        x = 2 * (i // 3)
+        start = pl.multiple_of((i % 3) * (6 * hid), 64)
+        rows = pl.ds(start, 8 * hid)
+        parts = [pair(h1, d, x + b, rows) for b in range(3) for d in range(3)]
+        hidden = gelu(mxu(wt2[...], jnp.concatenate(parts, axis=0))).astype(bf16)
+        for half in range(2):
+            h2[x + half, pl.ds(start, 6 * hid), :] = hidden[:, half * ny : half * ny + ny]
+        return carry
+
+    lax.fori_loop(0, 3 * ((nx + 2) // 2), second, 0)
+
+    for x in range(0, nx, 2):
+        parts = [
+            jnp.concatenate([h2[x + b, 0 : nz * hid, :], h2[x + b + 1, 0 : nz * hid, :]], axis=1)
+            for b in range(3)
+        ]
+        taps = mxu(wt3[...], jnp.concatenate(parts, axis=0))
+        for half in range(2):
+            o3[x + half] = taps[:, half * ny : half * ny + ny].reshape(nz, 8, ny)
+
+    sources = []
+    for part in range(2):
+        cells = []
+        for x in range(nx):
+            cells.append(
+                pol[part, x]
+                + (
+                    pltpu.roll(o3[x, :, part, :], 1, 1)
+                    + o3[x, :, 2 + part, :]
+                    + pltpu.roll(o3[x, :, 4 + part, :], ny - 1, 1)
+                )
+            )
+        sources.append(jnp.concatenate(cells, axis=1))
+    zk_high, zk_low = split(zk_ref[...])
+    both = [dot3(zk_high, zk_low, s) for s in sources]
+    lre = both[0][0:nz] - both[1][nz:]
+    lim = both[1][0:nz] + both[0][nz:]
+    lifted = []
+    for x in range(nx):
+        lifted.append(lre[:, x * ny : x * ny + ny])
+        lifted.append(lim[:, x * ny : x * ny + ny])
+    lifted = jnp.transpose(jnp.concatenate(lifted, axis=0))
+
+    lane = lax.broadcasted_iota(jnp.int32, (128, 128), 1)
+    real = (lane // nz) % 2 == 0
+    group = lax.broadcasted_iota(jnp.int32, (n, 128), 1) // (2 * nz)
+
+    def swap(x):
+        return jnp.where(real, pltpu.roll(x, 128 - nz, 1), -pltpu.roll(x, nz, 1))
+
+    def transform(index, x, other):
+        return dot3(tables_ref[index], tables_ref[index + 2], jnp.concatenate([x, other], axis=0))
+
+    def regroup(ref):
+        slabs = [ref[:, k, :] for k in range(4)]
+        blocks = []
+        for g in range(4):
+            block = slabs[0] if g == 0 else pltpu.roll(slabs[0], (-32 * g) % 128, 1)
+            for k in range(1, 4):
+                moved = slabs[k] if k == g else pltpu.roll(slabs[k], (32 * (k - g)) % 128, 1)
+                block = jnp.where(group == k, moved, block)
+            blocks.append(block)
+        return jnp.concatenate(blocks, axis=0)
+
+    def exchange(value, send, recv, send_sem, recv_sem):
+        for j in range(n):
+            send[j] = value[4 * j : 4 * j + 4, :]
+        recv[pl.ds(me, 1)] = send[pl.ds(me, 1)]
+
+        def copy(target, slot):
+            return pltpu.make_async_remote_copy(
+                src_ref=send.at[target],
+                dst_ref=recv.at[slot],
+                send_sem=send_sem.at[target],
+                recv_sem=recv_sem.at[slot],
+                device_id={"gx": target},
+                device_id_type=mesh_id,
+            )
+
+        def start(k, carry):
+            copy(lax.rem(me + k, n), me).start()
+            return carry
+
+        def finish(k, carry):
+            peer = lax.rem(me + n - k, n)
+            copy(peer, peer).wait_recv()
+            return carry
+
+        def sent(k, carry):
+            copy(lax.rem(me + k, n), me).wait_send()
+            return carry
+
+        lax.fori_loop(1, n, start, 0)
+        lax.fori_loop(1, n, finish, 0)
+        lax.fori_loop(1, n, sent, 0)
+
+    exchange(transform(0, lifted, swap(lifted)), send_a, recv_a, a_send, a_recv)
+
+    columns = regroup(recv_a)
+    spectrum = transform(1, columns, swap(columns))
+    weights = [
+        jnp.transpose(
+            jnp.concatenate(
+                [
+                    jnp.broadcast_to(spectral_ref[part, q : q + 1, :], (2 * nz, 128))
+                    for q in range(4)
+                ],
+                axis=0,
+            )
+        )
+        for part in range(2)
+    ]
+    scaled = weights[0] * spectrum - weights[1] * swap(spectrum)
+    exchange(transform(0, scaled, -swap(scaled)), send_b, recv_b, b_send, b_recv)
+
+    rows = regroup(recv_b)
+    result = jnp.transpose(transform(1, rows, -swap(rows))) * (1.0 / (128 * 128))
+    for x in range(nx):
+        for part in range(2):
+            first_row = (2 * x + part) * nz
+            out_ref[part, :, x, :] = (
+                incident_ref[part, :, x, :] + result[first_row : first_row + nz, :]
+            )
+
+
+def fused(mesh, incident, material, contrast, w_first, w_middle, w_last, z_kernel, spectral):
+    n = mesh.shape["gx"]
+    _, nz, nx, ny = incident.shape
+    hid = w_middle.shape[0]
+    f32, bf16 = jnp.float32, jnp.bfloat16
+    w1 = jnp.transpose(w_first, (2, 3, 4, 1, 0)).reshape(27, 4, hid)
+    w2 = jnp.transpose(w_middle, (2, 3, 4, 0, 1)).reshape(27, hid, hid)
+    w3 = jnp.transpose(w_last, (2, 3, 4, 0, 1)).reshape(27, 2, hid)
+    vmem = pl.BlockSpec(memory_space=pltpu.VMEM)
+    smem = pl.BlockSpec(memory_space=pltpu.SMEM)
+    dims = (n, nz, nx, ny, hid, contrast.shape[0])
+    dma = pltpu.SemaphoreType.DMA
+    return pl.pallas_call(
+        functools.partial(whole_kernel, dims),
+        out_shape=jax.ShapeDtypeStruct(incident.shape, f32),
+        in_specs=[vmem, vmem, smem] + [vmem] * 6,
+        out_specs=vmem,
+        scratch_shapes=[
+            pltpu.VMEM((10, 4, 16, 128), f32),
+            pltpu.VMEM((9, hid, 256), f32),
+            pltpu.VMEM((3, 8, 512), f32),
+            pltpu.VMEM((nz * hid, 640), bf16),
+            pltpu.VMEM((6 * hid, 9 * 256), bf16),
+            pltpu.VMEM((nz * 8, 3 * 512), bf16),
+            pltpu.VMEM((nx, 4 * nz, ny), bf16),
+            pltpu.VMEM((3, 4 * nz, ny), bf16),
+            pltpu.VMEM((3, 4 * nz, ny), bf16),
+            pltpu.VMEM((2, nx, nz, ny), f32),
+            pltpu.VMEM((3, nx + 6, 4 * nz, ny), bf16),
+            pltpu.VMEM((3, nx + 4, (nz + 4) * hid, ny), bf16),
+            pltpu.VMEM((nx + 2, (nz + 2) * hid, ny), bf16),
+            pltpu.VMEM((nx, nz, 8, ny), f32),
+            pltpu.VMEM((n, 4, 128), f32),
+            pltpu.VMEM((n, 4, 128), f32),
+            pltpu.VMEM((n, 4, 128), f32),
+            pltpu.VMEM((n, 4, 128), f32),
+            dma((2,)),
+            dma((2,)),
+            dma((n,)),
+            dma((n,)),
+            dma((n,)),
+            dma((n,)),
+        ],
+        compiler_params=pltpu.CompilerParams(
+            collective_id=0, has_side_effects=True, vmem_limit_bytes=40 << 20
+        ),
+    )(
+        incident,
+        material,
+        contrast,
+        w1,
+        w2,
+        w3,
+        z_kernel.reshape(2 * nz, nz),
+        spectral,
+        jnp.asarray(table_arrays(128, nx)),
+    )
+
+
+def body(mesh, incident, material, contrast, w_first, w_middle, w_last, z_kernel, spectral):
+    shapes_fit = (
+        incident.shape == (2, 16, 4, 128)
+        and mesh.shape["gx"] == 32
+        and mesh.shape["gy"] == 1
+        and w_middle.shape[0] == 32
+    )
+    args = (incident, material, contrast, w_first, w_middle, w_last, z_kernel, spectral)
+    return fused(mesh, *args) if shapes_fit else per_device(*args)
+
+
 def solution(mesh):
     placed = (
         P("grp", None, "gx", "gy"),
@@ -115,7 +510,7 @@
         P("grp", "gx", None),
     )
     return jax.shard_map(
-        per_device,
+        functools.partial(body, mesh),
         mesh=mesh,
         in_specs=placed,
         out_specs=P("grp", None, "gx", "gy"),

time: 268 us -> 37.3 us (0.14); the launches traced: 265 us -> 36.8 us
  matrix products: 213 us -> 0 us
  Pallas kernels: 0 us -> 29.8 us
  starting transfers between devices: 12.2 us -> 0 us
  waiting for transfers between devices: 9.39 us -> 0 us
  blocking collectives: 9.1 us -> 0 us
  local copies, waits for them, and re-layouts: 15 us -> 7.05 us
  other arithmetic: 5 us -> 0 us
    conv_general_dilated x3 -> x0, matrix products: 202 us -> none  [conv_layer(): lax.conv_general_dilated(values[None], weights, (1, 1, 1), ((1, 1), (0, 0...]
    pallas_call x0 -> x1, Pallas kernels: none -> 29.8 us  [fused(): pl.pallas_call(functools.partial(whole_kernel, dims), out_shape=jax.Shape...]
    dot_general x22 -> x0, matrix products: 11.2 us -> none  [the longest x1 0.94 us: per_device(): chi_im = jnp.einsum('k,kzxy->zxy', contrast[:, 1], selector, precision=high)]
    all_to_all x1 -> x0, blocking collectives: 9.1 us -> none  [green_apply(): rows = lax.all_to_all(spread, 'gx', split_axis=2, concat_axis=3, tiled=True)]
    conv_general_dilated x5 -> x0, local copies, waits for them, and re-layouts: 8.62 us -> none  [conv_layer(): lax.conv_general_dilated(values[None], weights, (1, 1, 1), ((1, 1), (0, 0...]
    all_to_all x1 -> x0, waiting for transfers between devices: 7.39 us -> none  [green_apply(): lax.all_to_all(jnp.stack([fwd_re, fwd_im]), 'gx', split_axis=3, concat_ax...]
    ppermute x4 -> x0, starting transfers between devices: 6.53 us -> none  [the longest x2 6 us: padded_2(): after = lax.ppermute(leading, axis, down)]
    all_to_all x1 -> x0, starting transfers between devices: 5.65 us -> none  [green_apply(): lax.all_to_all(jnp.stack([fwd_re, fwd_im]), 'gx', split_axis=3, concat_ax...]
  transfers between devices with their start and end apart: 5 -> 0, of which waited for: 2 -> 0; matrix products, arithmetic and copies ran while one was open for 0% -> 0% of each run, Pallas kernels for 0% -> 0%
where the time goes in v1:
time: 37.3 us; the launch traced here: 36.8 us
  Pallas kernels  29.8 us (80%)
  local copies, waits for them, and re-layouts  7.05 us (19%)
    pallas_call x1, Pallas kernels, fused(): pl.pallas_call(functools.partial(whole_kernel, dims), out_shape=jax.Shape...  29.8 us
    unnamed x20, local copies, waits for them, and re-layouts  7.05 us

profile of v1, /device:TPU:0, one launch (start us, length us, event | category | flops | bytes accessed | tf_op | source)
XLA Modules:
  0.0 36.8 jit_solution(15472960695772063045)
XLA Ops:
  0.0 0.0 copy-start.8
  0.0 0.0 copy-start.7
  0.0 0.7 %copy-done.8 = f32[8,2]{0,1:T(2,128)S(1)} copy-done((f32[8,2]{0,1:T(2,128)S(1)}, f32[8,2]{0,1:T(2,128)}, u32[]{:S(2)}) %copy-start.8) | copy-done | bytes 88
  0.7 0.1 copy.10.contrast_ref
  0.8 0.0 copy-done.7
  0.8 0.0 copy-start
  0.8 0.9 %copy-done = bf16[4,128,256]{2,1,0:T(8,128)(2,1)S(1)} copy-done((bf16[4,128,256]{2,1,0:T(8,128)(2,1)S(1)}, bf16[4,128,256]{2,1,0:T(8,128)(2,1)}, u32[]{:S(2)}) %copy-start) | copy-done | bytes 262168
  1.7 0.0 copy-start.1
  1.7 0.9 %copy-done.1 = bf16[32,32,3,3,3]{1,0,4,3,2:T(8,128)(2,1)S(1)} copy-done((bf16[32,32,3,3,3]{1,0,4,3,2:T(8,128)(2,1)S(1)}, bf16[32,32,3,3,3]{1,0,4,3,2:T(8,128)(2,1)}, u32[]{:S(2)}) %copy-start.1) | copy-done | bytes 55320
  2.7 0.0 copy-start.2
  2.7 0.8 %copy-done.2 = f32[2,16,4,128]{3,2,1,0:T(4,128)S(1)} copy-done((f32[2,16,4,128]{3,2,1,0:T(4,128)S(1)}, f32[2,16,4,128]{3,2,1,0:T(4,128)}, u32[]{:S(2)}) %copy-start.2) | copy-done | bytes 65560
  3.5 0.0 copy-start.3
  3.5 0.8 %copy-done.3 = s32[16,4,128]{2,1,0:T(4,128)S(1)} copy-done((s32[16,4,128]{2,1,0:T(4,128)S(1)}, s32[16,4,128]{2,1,0:T(4,128)}, u32[]{:S(2)}) %copy-start.3) | copy-done | bytes 32792
  4.2 0.0 copy-start.4
  4.3 0.7 %copy-done.4 = bf16[32,4,3,3,3]{0,1,4,3,2:T(4,128)(2,1)S(1)} copy-done((bf16[32,4,3,3,3]{0,1,4,3,2:T(4,128)(2,1)S(1)}, bf16[32,4,3,3,3]{0,1,4,3,2:T(4,128)(2,1)}, u32[]{:S(2)}) %copy-start.4) | copy-done | bytes 6936
  5.0 0.0 copy-start.5
  5.0 0.7 %copy-done.5 = f32[2,16,16]{2,1,0:T(8,128)S(1)} copy-done((f32[2,16,16]{2,1,0:T(8,128)S(1)}, f32[2,16,16]{2,1,0:T(8,128)}, u32[]{:S(2)}) %copy-start.5) | copy-done | bytes 2072
  5.7 0.0 copy-start.6
  5.7 0.7 %copy-done.6 = bf16[2,32,3,3,3]{1,0,4,3,2:T(2,128)(2,1)S(1)} copy-done((bf16[2,32,3,3,3]{1,0,4,3,2:T(2,128)(2,1)S(1)}, bf16[2,32,3,3,3]{1,0,4,3,2:T(2,128)(2,1)}, u32[]{:S(2)}) %copy-start.6) | copy-done | bytes 3480
  6.4 29.8 %shard_map.91 = f32[2,16,4,128]{3,2,1,0:T(4,128)S(1)} custom-call(f32[2,16,4,128]{3,2,1,0:T(4,128)S(1)} %copy-done.2, s32[16,4,128]{2,1,0:T(4,128)S(1)} %copy-done.3, f32[8,2]{1,0:T(8,128)S(1)} %copy.10.contrast_ref, bf16[27,4,32]{2,1,0:T(4,128)(2,1)S(1)} %bitcast.11, bf16[27,32,32]{2,1,0:T(8,128)(2,1)S(1)} %bitcast.10, bf16[27,2,32]{2,1,0:T(2,128)(2,1)S(1)} %bitcast.13, ...), custom_call_target="tpu_custom_call" | custom-call | tf_op jit(solution)/shard_map/pallas_call | solution.py:443
  36.2 0.6 %copy.12 = f32[2,16,4,128]{3,2,1,0:T(4,128)} copy(f32[2,16,4,128]{3,2,1,0:T(4,128)S(1)} %shard_map.91) | data formatting | bytes 131072
Async XLA Ops:
  0.0 0.7 %copy-start.8 = (f32[8,2]{0,1:T(2,128)S(1)}, f32[8,2]{0,1:T(2,128)}, u32[]{:S(2)}) copy-start(f32[8,2]{0,1:T(2,128)} %param.11) | copy-start | bytes 196
  0.0 0.8 %copy-start.7 = (f32[2,4,128]{2,1,0:T(4,128)S(1)}, f32[2,4,128]{2,1,0:T(4,128)}, u32[]{:S(2)}) copy-start(f32[2,4,128]{2,1,0:T(4,128)} %spectral_ref.1) | copy-start | bytes 12292
  0.8 1.0 %copy-start = (bf16[4,128,256]{2,1,0:T(8,128)(2,1)S(1)}, bf16[4,128,256]{2,1,0:T(8,128)(2,1)}, u32[]{:S(2)}) copy-start(bf16[4,128,256]{2,1,0:T(8,128)(2,1)} %constant.2.clone.tables_ref) | copy-start | bytes 786436
  1.7 0.9 %copy-start.1 = (bf16[32,32,3,3,3]{1,0,4,3,2:T(8,128)(2,1)S(1)}, bf16[32,32,3,3,3]{1,0,4,3,2:T(8,128)(2,1)}, u32[]{:S(2)}) copy-start(bf16[32,32,3,3,3]{1,0,4,3,2:T(8,128)(2,1)} %param.13) | copy-start | bytes 165892
  2.7 0.8 %copy-start.2 = (f32[2,16,4,128]{3,2,1,0:T(4,128)S(1)}, f32[2,16,4,128]{3,2,1,0:T(4,128)}, u32[]{:S(2)}) copy-start(f32[2,16,4,128]{3,2,1,0:T(4,128)} %incident_ref.1) | copy-start | bytes 196612
  3.5 0.8 %copy-start.3 = (s32[16,4,128]{2,1,0:T(4,128)S(1)}, s32[16,4,128]{2,1,0:T(4,128)}, u32[]{:S(2)}) copy-start(s32[16,4,128]{2,1,0:T(4,128)} %material_ref.1) | copy-start | bytes 98308
  4.2 0.7 %copy-start.4 = (bf16[32,4,3,3,3]{0,1,4,3,2:T(4,128)(2,1)S(1)}, bf16[32,4,3,3,3]{0,1,4,3,2:T(4,128)(2,1)}, u32[]{:S(2)}) copy-start(bf16[32,4,3,3,3]{0,1,4,3,2:T(4,128)(2,1)} %param.12) | copy-start | bytes 20740
  5.0 0.7 %copy-start.5 = (f32[2,16,16]{2,1,0:T(8,128)S(1)}, f32[2,16,16]{2,1,0:T(8,128)}, u32[]{:S(2)}) copy-start(f32[2,16,16]{2,1,0:T(8,128)} %param.15) | copy-start | bytes 6148
  5.7 0.7 %copy-start.6 = (bf16[2,32,3,3,3]{1,0,4,3,2:T(2,128)(2,1)S(1)}, bf16[2,32,3,3,3]{1,0,4,3,2:T(2,128)(2,1)}, u32[]{:S(2)}) copy-start(bf16[2,32,3,3,3]{1,0,4,3,2:T(2,128)(2,1)} %param.14) | copy-start | bytes 10372

commit v2 on v1

--- a/solution.py
+++ b/solution.py
@@ -144,6 +144,16 @@
 
 def whole_kernel(
     dims,
+    incident_hbm,
+    material_hbm,
+    contrast_hbm,
+    w1_hbm,
+    w2_hbm,
+    w3_hbm,
+    zk_hbm,
+    spectral_hbm,
+    tables_hbm,
+    out_ref,
     incident_ref,
     material_ref,
     contrast_ref,
@@ -153,7 +163,7 @@
     zk_ref,
     spectral_ref,
     tables_ref,
-    out_ref,
+    load_sem,
     base1,
     base2,
     base3,
@@ -185,6 +195,23 @@
     right, left = lax.rem(me + 1, n), lax.rem(me + n - 1, n)
     mesh_id = pl.DeviceIdType.MESH
 
+    pairs = (
+        (incident_hbm, incident_ref),
+        (material_hbm, material_ref),
+        (contrast_hbm, contrast_ref),
+        (w1_hbm, w1_ref),
+        (w2_hbm, w2_ref),
+        (w3_hbm, w3_ref),
+        (zk_hbm, zk_ref),
+        (spectral_hbm, spectral_ref),
+        (tables_hbm, tables_ref),
+    )
+    loads = [
+        pltpu.make_async_copy(src, dst, load_sem.at[k]) for k, (src, dst) in enumerate(pairs)
+    ]
+    for load in loads:
+        load.start()
+
     barrier = pltpu.get_barrier_semaphore()
 
     def greet(k, carry):
@@ -193,7 +220,10 @@
         )
         return carry
 
-    lax.fori_loop(1, n, greet, 0)
+    lax.fori_loop(1, n, greet, 0, unroll=True)
+
+    for load in loads[:3]:
+        load.wait()
 
     for x in range(nx):
         f0 = incident_ref[0, :, x, :]
@@ -203,8 +233,8 @@
         ci = jnp.zeros_like(f0)
         for k in range(classes):
             hit = mat == k
-            cr = jnp.where(hit, contrast_ref[k, 0], cr)
-            ci = jnp.where(hit, contrast_ref[k, 1], ci)
+            cr = jnp.where(hit, contrast_ref[0:1, k : k + 1], cr)
+            ci = jnp.where(hit, contrast_ref[1:2, k : k + 1], ci)
         pr = cr * f0 - ci * f1
         pi = cr * f1 + ci * f0
         pol[0, x] = pr
@@ -232,6 +262,8 @@
     to_right.start()
     to_left.start()
 
+    for load in loads[3:]:
+        load.wait()
     base1[...] = jnp.zeros_like(base1)
     base2[...] = jnp.zeros_like(base2)
     base3[...] = jnp.zeros_like(base3)
@@ -372,32 +404,23 @@
             send[j] = value[4 * j : 4 * j + 4, :]
         recv[pl.ds(me, 1)] = send[pl.ds(me, 1)]
 
-        def copy(target, slot):
-            return pltpu.make_async_remote_copy(
+        def start(k, carry):
+            target = lax.rem(me + k, n)
+            pltpu.make_async_remote_copy(
                 src_ref=send.at[target],
-                dst_ref=recv.at[slot],
-                send_sem=send_sem.at[target],
-                recv_sem=recv_sem.at[slot],
+                dst_ref=recv.at[me],
+                send_sem=send_sem,
+                recv_sem=recv_sem,
                 device_id={"gx": target},
                 device_id_type=mesh_id,
-            )
-
-        def start(k, carry):
-            copy(lax.rem(me + k, n), me).start()
+            ).start()
             return carry
 
-        def finish(k, carry):
-            peer = lax.rem(me + n - k, n)
-            copy(peer, peer).wait_recv()
-            return carry
-
-        def sent(k, carry):
-            copy(lax.rem(me + k, n), me).wait_send()
-            return carry
-
-        lax.fori_loop(1, n, start, 0)
-        lax.fori_loop(1, n, finish, 0)
-        lax.fori_loop(1, n, sent, 0)
+        lax.fori_loop(1, n, start, 0, unroll=True)
+        wait_all(recv, recv_sem)
+
+    def wait_all(ref, sem):
+        pltpu.make_async_copy(ref.at[pl.ds(0, n - 1)], ref.at[pl.ds(0, n - 1)], sem).wait()
 
     exchange(transform(0, lifted, swap(lifted)), send_a, recv_a, a_send, a_recv)
 
@@ -426,6 +449,8 @@
             out_ref[part, :, x, :] = (
                 incident_ref[part, :, x, :] + result[first_row : first_row + nz, :]
             )
+    wait_all(send_a, a_send)
+    wait_all(send_b, b_send)
 
 
 def fused(mesh, incident, material, contrast, w_first, w_middle, w_last, z_kernel, spectral):
@@ -437,15 +462,28 @@
     w2 = jnp.transpose(w_middle, (2, 3, 4, 0, 1)).reshape(27, hid, hid)
     w3 = jnp.transpose(w_last, (2, 3, 4, 0, 1)).reshape(27, 2, hid)
     vmem = pl.BlockSpec(memory_space=pltpu.VMEM)
-    smem = pl.BlockSpec(memory_space=pltpu.SMEM)
+    hbm = pl.BlockSpec(memory_space=pltpu.HBM)
     dims = (n, nz, nx, ny, hid, contrast.shape[0])
     dma = pltpu.SemaphoreType.DMA
+    operands = (
+        incident,
+        material,
+        contrast.T,
+        w1,
+        w2,
+        w3,
+        z_kernel.reshape(2 * nz, nz),
+        spectral,
+        jnp.asarray(table_arrays(128, nx)),
+    )
     return pl.pallas_call(
         functools.partial(whole_kernel, dims),
         out_shape=jax.ShapeDtypeStruct(incident.shape, f32),
-        in_specs=[vmem, vmem, smem] + [vmem] * 6,
+        in_specs=[hbm] * len(operands),
         out_specs=vmem,
-        scratch_shapes=[
+        scratch_shapes=[pltpu.VMEM(x.shape, x.dtype) for x in operands]
+        + [
+            dma((len(operands),)),
             pltpu.VMEM((10, 4, 16, 128), f32),
             pltpu.VMEM((9, hid, 256), f32),
             pltpu.VMEM((3, 8, 512), f32),
@@ -466,25 +504,15 @@
             pltpu.VMEM((n, 4, 128), f32),
             dma((2,)),
             dma((2,)),
-            dma((n,)),
-            dma((n,)),
-            dma((n,)),
-            dma((n,)),
+            dma,
+            dma,
+            dma,
+            dma,
         ],
         compiler_params=pltpu.CompilerParams(
-            collective_id=0, has_side_effects=True, vmem_limit_bytes=40 << 20
+            collective_id=0, has_side_effects=True
         ),
-    )(
-        incident,
-        material,
-        contrast,
-        w1,
-        w2,
-        w3,
-        z_kernel.reshape(2 * nz, nz),
-        spectral,
-        jnp.asarray(table_arrays(128, nx)),
-    )
+    )(*operands)
 
 
 def body(mesh, incident, material, contrast, w_first, w_middle, w_last, z_kernel, spectral):

time: 37.3 us -> 29.8 us (0.80)
  local copies, waits for them, and re-layouts: 7.05 us -> 1.47 us
  Pallas kernels: 29.8 us -> 28.1 us
    unnamed x20 -> x1, local copies, waits for them, and re-layouts: 7.05 us -> 1.47 us
    pallas_call x1, Pallas kernels: 29.8 us -> 28.1 us  [fused(): pl.pallas_call(functools.partial(whole_kernel, dims), out_shape=jax.Shape...]
where the time goes in v2:
time: 29.8 us; the launch traced here: 29.6 us
  Pallas kernels  28.1 us (94%)
  local copies, waits for them, and re-layouts  1.47 us (5%)
    pallas_call x1, Pallas kernels, fused(): pl.pallas_call(functools.partial(whole_kernel, dims), out_shape=jax.Shape...  28.1 us
    unnamed x1, local copies, waits for them, and re-layouts  1.47 us

profile of v2, /device:TPU:0, one launch (start us, length us, event | category | flops | bytes accessed | tf_op | source)
XLA Modules:
  0.0 29.6 jit_solution(13518793771726648551)
XLA Ops:
  0.0 28.1 %shard_map.91 = f32[2,16,4,128]{3,2,1,0:T(4,128)} custom-call(f32[2,16,4,128]{3,2,1,0:T(4,128)} %incident_hbm.1, s32[16,4,128]{2,1,0:T(4,128)} %material_hbm.1, f32[2,8]{1,0:T(2,128)} %bitcast.15, bf16[27,4,32]{2,1,0:T(4,128)(2,1)} %bitcast.12, bf16[27,32,32]{2,1,0:T(8,128)(2,1)} %bitcast.11, bf16[27,2,32]{2,1,0:T(2,128)(2,1)} %bitcast.14, ...), custom_call_target="tpu_custom_call" | custom-call | tf_op jit(solution)/shard_map/pallas_call | solution.py:479
  28.1 1.5 %copy.11 = f32[2,16,4,128]{3,2,1,0:T(4,128)} copy(f32[2,16,4,128]{3,2,1,0:T(4,128)} %shard_map.91) | data formatting | bytes 131072

commit v3 on v2

--- a/solution.py
+++ b/solution.py
@@ -178,6 +178,7 @@
     h1,
     h2,
     o3,
+    scale,
     send_a,
     recv_a,
     send_b,
@@ -304,35 +305,57 @@
     h1[:, :, 0:hid, :] = jnp.zeros((3, nx + 4, hid, ny), bf16)
     h1[:, :, (nz + 1) * hid :, :] = jnp.zeros((3, nx + 4, 3 * hid, ny), bf16)
 
+    def shifted(x):
+        return pltpu.roll(x, 1, 1), x, pltpu.roll(x, ny - 1, 1)
+
+    def pair(ref, d, x, rows):
+        return jnp.concatenate([ref[d, x, rows, :], ref[d, x + 1, rows, :]], axis=1)
+
+    def place(x, piece):
+        for d, moved in enumerate(shifted(piece.astype(f32))):
+            feat[d, x] = moved.astype(bf16)
+
+    def first(x, other):
+        parts = [
+            jnp.concatenate([feat[d, x + b], feat[d, other + b]], axis=1)
+            for b in range(3)
+            for d in range(3)
+        ]
+        hidden = gelu(mxu(wt1[...], jnp.concatenate(parts + [parts[0]], axis=0)))
+        for half, cell in enumerate((x, other)):
+            for d, moved in enumerate(shifted(hidden[:, half * ny : half * ny + ny])):
+                h1[d, cell, hid : (nz + 1) * hid, :] = moved.astype(bf16)
+
+    for x in range(nx):
+        place(x + 3, own[x])
+    first(3, 4)
+    weights = [
+        jnp.transpose(
+            jnp.concatenate(
+                [
+                    jnp.broadcast_to(spectral_ref[part, q : q + 1, :], (2 * nz, 128))
+                    for q in range(4)
+                ],
+                axis=0,
+            )
+        )
+        for part in range(2)
+    ]
+    for part in range(2):
+        scale[part] = weights[part]
+
     to_right.wait()
     to_left.wait()
 
-    def shifted(x):
-        return pltpu.roll(x, 1, 1), x, pltpu.roll(x, ny - 1, 1)
-
-    for x in range(nx + 6):
-        if x < 3:
-            piece = halo_left[x]
-        elif x < nx + 3:
-            piece = own[x - 3]
-        else:
-            piece = halo_right[x - nx - 3]
-        for d, moved in enumerate(shifted(piece.astype(f32))):
-            feat[d, x] = moved.astype(bf16)
-
-    def pair(ref, d, x, rows):
-        return jnp.concatenate([ref[d, x, rows, :], ref[d, x + 1, rows, :]], axis=1)
-
-    def first(i, carry):
-        x = 2 * i
-        parts = [pair(feat, d, x + b, slice(None)) for b in range(3) for d in range(3)]
-        hidden = gelu(mxu(wt1[...], jnp.concatenate(parts + [parts[0]], axis=0)))
-        for half in range(2):
-            for d, moved in enumerate(shifted(hidden[:, half * ny : half * ny + ny])):
-                h1[d, x + half, hid : (nz + 1) * hid, :] = moved.astype(bf16)
+    for x in range(3):
+        place(x, halo_left[x])
+        place(x + nx + 3, halo_right[x])
+
+    def outer(i, carry):
+        first(2 - i, 5 + i)
         return carry
 
-    lax.fori_loop(0, (nx + 4) // 2, first, 0)
+    lax.fori_loop(0, 3, outer, 0, unroll=True)
 
     def second(i, carry):
         x = 2 * (i // 3)
@@ -344,7 +367,7 @@
             h2[x + half, pl.ds(start, 6 * hid), :] = hidden[:, half * ny : half * ny + ny]
         return carry
 
-    lax.fori_loop(0, 3 * ((nx + 2) // 2), second, 0)
+    lax.fori_loop(0, 3 * ((nx + 2) // 2), second, 0, unroll=True)
 
     for x in range(0, nx, 2):
         parts = [
@@ -426,19 +449,7 @@
 
     columns = regroup(recv_a)
     spectrum = transform(1, columns, swap(columns))
-    weights = [
-        jnp.transpose(
-            jnp.concatenate(
-                [
-                    jnp.broadcast_to(spectral_ref[part, q : q + 1, :], (2 * nz, 128))
-                    for q in range(4)
-                ],
-                axis=0,
-            )
-        )
-        for part in range(2)
-    ]
-    scaled = weights[0] * spectrum - weights[1] * swap(spectrum)
+    scaled = scale[0] * spectrum - scale[1] * swap(spectrum)
     exchange(transform(0, scaled, -swap(scaled)), send_b, recv_b, b_send, b_recv)
 
     rows = regroup(recv_b)
@@ -498,6 +509,7 @@
             pltpu.VMEM((3, nx + 4, (nz + 4) * hid, ny), bf16),
             pltpu.VMEM((nx + 2, (nz + 2) * hid, ny), bf16),
             pltpu.VMEM((nx, nz, 8, ny), f32),
+            pltpu.VMEM((2, 128, 128), f32),
             pltpu.VMEM((n, 4, 128), f32),
             pltpu.VMEM((n, 4, 128), f32),
             pltpu.VMEM((n, 4, 128), f32),
@@ -510,9 +522,9 @@
             dma,
         ],
         compiler_params=pltpu.CompilerParams(
-            collective_id=0, has_side_effects=True
+            collective_id=0, has_side_effects=True, vmem_limit_bytes=40 << 20
         ),
-    )(*operands)
+    )(*[pltpu.with_memory_space_constraint(x, pltpu.HBM) for x in operands])
 
 
 def body(mesh, incident, material, contrast, w_first, w_middle, w_last, z_kernel, spectral):

time: 29.8 us -> 25.6 us (0.86)
  Pallas kernels: 28.1 us -> 24.8 us
  local copies, waits for them, and re-layouts: 1.47 us -> 0.63 us
    pallas_call x1, Pallas kernels: 28.1 us -> 24.8 us  [fused(): pl.pallas_call(functools.partial(whole_kernel, dims), out_shape=jax.Shape...]
    unnamed x1, local copies, waits for them, and re-layouts: 1.47 us -> 0.63 us
where the time goes in v3:
time: 25.6 us; the launch traced here: 25.5 us
  Pallas kernels  24.8 us (97%)
  local copies, waits for them, and re-layouts  0.63 us (2%)
    pallas_call x1, Pallas kernels, fused(): pl.pallas_call(functools.partial(whole_kernel, dims), out_shape=jax.Shape...  24.8 us
    unnamed x1, local copies, waits for them, and re-layouts  0.63 us

profile of v3, /device:TPU:0, one launch (start us, length us, event | category | flops | bytes accessed | tf_op | source)
XLA Modules:
  0.0 25.5 jit_solution(9337729957946970107)
XLA Ops:
  0.0 24.8 %shard_map.91 = f32[2,16,4,128]{3,2,1,0:T(4,128)S(1)} custom-call(f32[2,16,4,128]{3,2,1,0:T(4,128)} %incident_hbm.1, s32[16,4,128]{2,1,0:T(4,128)} %material_hbm.1, f32[2,8]{1,0:T(2,128)} %bitcast.15, bf16[27,4,32]{2,1,0:T(4,128)(2,1)} %bitcast.12, bf16[27,32,32]{2,1,0:T(8,128)(2,1)} %bitcast.11, bf16[27,2,32]{2,1,0:T(2,128)(2,1)} %bitcast.14, ...), custom_call_target="tpu_custom_call" | custom-call | tf_op jit(solution)/shard_map/pallas_call | solution.py:490
  24.8 0.6 %copy.11 = f32[2,16,4,128]{3,2,1,0:T(4,128)} copy(f32[2,16,4,128]{3,2,1,0:T(4,128)S(1)} %shard_map.91) | data formatting | bytes 131072
